TPU v7x, 32 devices: a whole 2x2x4 slice. The times are simulated.
32 devices in a mesh: expert: 8 (over y, x, core), token: 4 (over z).
Axes of the slice: x: 2, y: 2, z: 4, core: 2. Of those that a mesh axis runs over, the one named last changes fastest.
Arguments:
- activations: bfloat16 [16, 1024, 768], P('expert', 'token'), may hold values from -6 to 6
- routed: int32 [16, 1024], P('expert', 'token'), may hold values 0 or 1
- weights: bfloat16 [128, 768, 256], P(('expert', 'token')), may hold values from -6 to 6, as said below
- kept_mask: int32 [128, 768, 256], P(('expert', 'token')), may hold values 0 or 1
- step_counts: int32 [128], P(('expert', 'token')), may hold values from 1 to 7
- ridge_scale: float32 [128], P(('expert', 'token')), may hold values from 0.05 to 0.5
Outputs:
- rebuilt: float32 [128, 768, 256], P(('expert', 'token'))
- misfit: float32 [16], P('expert')
Inputs may be any that keep to these rules, and one draw needn't show every extreme that they name: `weights`: every entry's magnitude is at least 0.25.
All inputs are finite; a program needn't handle non-finite values. No bound on the sum of `routed` or of `kept_mask` on one device may be relied on, other than what follows from the above.
Results may differ from a plain program's by a relative error of at most 0.0003.
Values may be sent and summed in bfloat16 or wider, within the bound.
A program may use at most 64 MiB of HBM per device.

v0:
```python
import jax
import jax.numpy as jnp
from jax import lax
from jax.sharding import PartitionSpec as P

D = 2048
COLS = 256


def solve_task(gram_matrix, frobenius, task_weights, task_mask, task_count, task_ridge):
    float_weights = task_weights.astype(jnp.float32)
    float_mask = task_mask.astype(jnp.float32)
    damping = task_ridge * frobenius
    step_size = 1.0 / (frobenius + damping)

    def advance(turn_index, current):
        gradient = (
            jnp.dot(gram_matrix, current - float_weights, precision=lax.Precision.HIGHEST)
            + damping * current
        )
        return current - step_size * (float_mask * gradient)

    result = lax.fori_loop(0, task_count, advance, float_mask * float_weights)
    change = result - float_weights
    numerator = jnp.sum(change * jnp.dot(gram_matrix, change, precision=lax.Precision.HIGHEST))
    energy = jnp.sum(
        float_weights * jnp.dot(gram_matrix, float_weights, precision=lax.Precision.HIGHEST)
    )
    return (result, numerator, energy)


def on_device(activations, routed, weights, kept_mask, step_counts, ridge_scale):
    local_experts, row_count, features = activations.shape
    local_tasks = weights.shape[0]
    per_expert = D // COLS
    total_rows = row_count * lax.axis_size("token")
    own_slot = lax.axis_index("token") * local_tasks // per_expert
    masked = activations * routed[:, :, None].astype(jnp.bfloat16)
    own_rows = lax.dynamic_index_in_dim(
        lax.all_gather(masked, "token", axis=1, tiled=True), own_slot, 0, keepdims=False
    )
    gram_sum = lax.dot_general(
        own_rows, own_rows, (((0,), (0,)), ((), ())), preferred_element_type=jnp.float32
    )
    gram_matrix = gram_sum / total_rows
    frobenius = jnp.sqrt(jnp.sum(gram_matrix * gram_matrix))

    def one_task(task_args):
        task_weights, task_mask, task_count, task_ridge = task_args
        return solve_task(gram_matrix, frobenius, task_weights, task_mask, task_count, task_ridge)

    rebuilt, numerators, energies = lax.map(
        one_task, (weights, kept_mask, step_counts, ridge_scale)
    )
    picker = (jnp.arange(local_experts) == own_slot).astype(jnp.float32)
    expert_terms = lax.psum(picker * jnp.sum(numerators), "token")
    layer_energy = lax.psum(jnp.sum(energies), ("expert", "token"))
    expert_total = local_experts * lax.axis_size("expert")
    misfit = expert_terms / (layer_energy / expert_total + 1e-06)
    return (rebuilt, misfit)


def solution(mesh):
    placed = (
        P("expert", "token", None),
        P("expert", "token"),
        P(("expert", "token"), None, None),
        P(("expert", "token"), None, None),
        P(("expert", "token")),
        P(("expert", "token")),
    )
    return jax.shard_map(
        on_device,
        mesh=mesh,
        in_specs=placed,
        out_specs=(P(("expert", "token"), None, None), P("expert")),
        check_vma=False,
    )
```

profile of v0, /device:TPU:0, one launch (start us, length us, event | category | flops | bytes accessed | tf_op | source)
XLA Modules:
  0.0 320.7 jit_solution(10718532296523301616)
XLA Ops:
  7.9 2.1 broadcast_multiply_fusion
  10.2 66.2 %all-gather.2.cloned.1.call-done = bf16[2,1024,768]{2,1,0:T(8,128)(2,1)} async-done(((bf16[2,256,768]{2,1,0:T(8,128)(2,1)}), bf16[2,1024,768]{2,1,0:T(8,128)(2,1)}) %all-gather.2.cloned.1.call-update) | async-done | bytes 3145744 | tf_op jit(solution)/shard_map/all_gather | solution.py:40
  76.4 4.1 %multiply_reduce_fusion = (f32[]{:T(128)}, f32[768,768]{1,0:T(8,128)S(1)}) fusion(bf16[2,1024,768]{2,1,0:T(8,128)(2,1)} %all-gather.2.cloned.1.call-done, s32[]{:T(128)S(6)} %select_n.10), kind=kOutput, calls=%fused_computation.22 | convolution fusion | flops 1209729024 | bytes 3932168 | tf_op jit(solution)/shard_map/dot_general | solution.py:42
  81.1 163.0 %while.25 = (s32[]{:T(128)}, f32[4,768,256]{2,1,0:T(8,128)}, f32[4]{0:T(128)S(1)}, f32[4]{0:T(128)S(1)}, s32[4,768,256]{2,1,0:T(8,128)}, /*index=5*/bf16[4,768,2...) while((s32[]{:T(128)}, f32[4,768,256]{2,1,0:T(8,128)}, ...), condition=%wide.region_6.7_spmd, body=%wide.region_1.6_spmd.sunk | while | flops 5439750144 | bytes 29491652 | solution.py:52
  84.1 2.2 fusion.35
  88.1 2.1 constant_dynamic-slice_fusion.5
  90.2 1.4 copy.22
  94.6 27.0 %while.26 = (s32[]{:T(128)}, f32[768,256]{0,1:T(8,128)S(1)}, s32[]{:T(128)}, f32[]{:T(128)}, f32[768,256]{0,1:T(8,128)}, /*index=5*/f32[768,768]{1,0:T(8,128)S(1)}, f32[]{:T(128)}, f32[768,256]{0,1:T(8,128)}, s32[]{:T(128)}) while((s32[]{:T(128)}, f32[768,256]{0,1:T(8,128)S(1)}, s32[]{:T(128)}, f32[]{:T(128)}, f32[768,256]{0,1:T(8,128)}, ...), condition=%wide.region_3.3_spmd, body=%wide.region_2.2_spmd.sunk | while | flops 1813118976 | bytes 7077989 | solution.py:23
  95.3 3.7 %fusion.38 = f32[768,256]{0,1:T(8,128)S(1)} fusion(f32[768,256]{0,1:T(8,128)S(1)} %copy.48, f32[768,256]{0,1:T(8,128)} %get-tuple-element.307, f32[768,768]{1,0:T(8,128)S(1)} %get-tuple-element.305, f32[768,256]{0,1:T(8,128)} %get-tuple-element.304, f32[]{:T(128)} %get-tuple-element.306, f32[]{:T(128)} %get-tuple-element.303), kind=kOutput, calls=%fused_computation.4.clone.1 | convolution fusion | flops 1813118976 | bytes 5505032 | tf_op jit(solution)/shard_map/while/body/eval_jaxpr/while/body/dot_general | solution.py:18
  99.7 3.7 %fusion.38 = f32[768,256]{0,1:T(8,128)S(1)} fusion(f32[768,256]{0,1:T(8,128)S(1)} %copy.48, f32[768,256]{0,1:T(8,128)} %get-tuple-element.307, f32[768,768]{1,0:T(8,128)S(1)} %get-tuple-element.305, f32[768,256]{0,1:T(8,128)} %get-tuple-element.304, f32[]{:T(128)} %get-tuple-element.306, f32[]{:T(128)} %get-tuple-element.303), kind=kOutput, calls=%fused_computation.4.clone.1 | convolution fusion | flops 1813118976 | bytes 5505032 | tf_op jit(solution)/shard_map/while/body/eval_jaxpr/while/body/dot_general | solution.py:18
  104.1 3.7 %fusion.38 = f32[768,256]{0,1:T(8,128)S(1)} fusion(f32[768,256]{0,1:T(8,128)S(1)} %copy.48, f32[768,256]{0,1:T(8,128)} %get-tuple-element.307, f32[768,768]{1,0:T(8,128)S(1)} %get-tuple-element.305, f32[768,256]{0,1:T(8,128)} %get-tuple-element.304, f32[]{:T(128)} %get-tuple-element.306, f32[]{:T(128)} %get-tuple-element.303), kind=kOutput, calls=%fused_computation.4.clone.1 | convolution fusion | flops 1813118976 | bytes 5505032 | tf_op jit(solution)/shard_map/while/body/eval_jaxpr/while/body/dot_general | solution.py:18
  108.5 3.7 %fusion.38 = f32[768,256]{0,1:T(8,128)S(1)} fusion(f32[768,256]{0,1:T(8,128)S(1)} %copy.48, f32[768,256]{0,1:T(8,128)} %get-tuple-element.307, f32[768,768]{1,0:T(8,128)S(1)} %get-tuple-element.305, f32[768,256]{0,1:T(8,128)} %get-tuple-element.304, f32[]{:T(128)} %get-tuple-element.306, f32[]{:T(128)} %get-tuple-element.303), kind=kOutput, calls=%fused_computation.4.clone.1 | convolution fusion | flops 1813118976 | bytes 5505032 | tf_op jit(solution)/shard_map/while/body/eval_jaxpr/while/body/dot_general | solution.py:18
  112.9 3.7 %fusion.38 = f32[768,256]{0,1:T(8,128)S(1)} fusion(f32[768,256]{0,1:T(8,128)S(1)} %copy.48, f32[768,256]{0,1:T(8,128)} %get-tuple-element.307, f32[768,768]{1,0:T(8,128)S(1)} %get-tuple-element.305, f32[768,256]{0,1:T(8,128)} %get-tuple-element.304, f32[]{:T(128)} %get-tuple-element.306, f32[]{:T(128)} %get-tuple-element.303), kind=kOutput, calls=%fused_computation.4.clone.1 | convolution fusion | flops 1813118976 | bytes 5505032 | tf_op jit(solution)/shard_map/while/body/eval_jaxpr/while/body/dot_general | solution.py:18
  117.3 3.7 %fusion.38 = f32[768,256]{0,1:T(8,128)S(1)} fusion(f32[768,256]{0,1:T(8,128)S(1)} %copy.48, f32[768,256]{0,1:T(8,128)} %get-tuple-element.307, f32[768,768]{1,0:T(8,128)S(1)} %get-tuple-element.305, f32[768,256]{0,1:T(8,128)} %get-tuple-element.304, f32[]{:T(128)} %get-tuple-element.306, f32[]{:T(128)} %get-tuple-element.303), kind=kOutput, calls=%fused_computation.4.clone.1 | convolution fusion | flops 1813118976 | bytes 5505032 | tf_op jit(solution)/shard_map/while/body/eval_jaxpr/while/body/dot_general | solution.py:18
  121.6 2.9 fusion.34
  126.4 2.1 constant_dynamic-update-slice_fusion.2
  131.5 2.2 fusion.35
  135.4 2.1 constant_dynamic-slice_fusion.5
  137.5 1.4 copy.22
  142.0 27.0 %while.26 = (s32[]{:T(128)}, f32[768,256]{0,1:T(8,128)S(1)}, s32[]{:T(128)}, f32[]{:T(128)}, f32[768,256]{0,1:T(8,128)}, /*index=5*/f32[768,768]{1,0:T(8,128)S(1)}, f32[]{:T(128)}, f32[768,256]{0,1:T(8,128)}, s32[]{:T(128)}) while((s32[]{:T(128)}, f32[768,256]{0,1:T(8,128)S(1)}, s32[]{:T(128)}, f32[]{:T(128)}, f32[768,256]{0,1:T(8,128)}, ...), condition=%wide.region_3.3_spmd, body=%wide.region_2.2_spmd.sunk | while | flops 1813118976 | bytes 7077989 | solution.py:23
  142.7 3.7 %fusion.38 = f32[768,256]{0,1:T(8,128)S(1)} fusion(f32[768,256]{0,1:T(8,128)S(1)} %copy.48, f32[768,256]{0,1:T(8,128)} %get-tuple-element.307, f32[768,768]{1,0:T(8,128)S(1)} %get-tuple-element.305, f32[768,256]{0,1:T(8,128)} %get-tuple-element.304, f32[]{:T(128)} %get-tuple-element.306, f32[]{:T(128)} %get-tuple-element.303), kind=kOutput, calls=%fused_computation.4.clone.1 | convolution fusion | flops 1813118976 | bytes 5505032 | tf_op jit(solution)/shard_map/while/body/eval_jaxpr/while/body/dot_general | solution.py:18
  147.1 3.7 %fusion.38 = f32[768,256]{0,1:T(8,128)S(1)} fusion(f32[768,256]{0,1:T(8,128)S(1)} %copy.48, f32[768,256]{0,1:T(8,128)} %get-tuple-element.307, f32[768,768]{1,0:T(8,128)S(1)} %get-tuple-element.305, f32[768,256]{0,1:T(8,128)} %get-tuple-element.304, f32[]{:T(128)} %get-tuple-element.306, f32[]{:T(128)} %get-tuple-element.303), kind=kOutput, calls=%fused_computation.4.clone.1 | convolution fusion | flops 1813118976 | bytes 5505032 | tf_op jit(solution)/shard_map/while/body/eval_jaxpr/while/body/dot_general | solution.py:18
  151.5 3.7 %fusion.38 = f32[768,256]{0,1:T(8,128)S(1)} fusion(f32[768,256]{0,1:T(8,128)S(1)} %copy.48, f32[768,256]{0,1:T(8,128)} %get-tuple-element.307, f32[768,768]{1,0:T(8,128)S(1)} %get-tuple-element.305, f32[768,256]{0,1:T(8,128)} %get-tuple-element.304, f32[]{:T(128)} %get-tuple-element.306, f32[]{:T(128)} %get-tuple-element.303), kind=kOutput, calls=%fused_computation.4.clone.1 | convolution fusion | flops 1813118976 | bytes 5505032 | tf_op jit(solution)/shard_map/while/body/eval_jaxpr/while/body/dot_general | solution.py:18
  155.8 3.7 %fusion.38 = f32[768,256]{0,1:T(8,128)S(1)} fusion(f32[768,256]{0,1:T(8,128)S(1)} %copy.48, f32[768,256]{0,1:T(8,128)} %get-tuple-element.307, f32[768,768]{1,0:T(8,128)S(1)} %get-tuple-element.305, f32[768,256]{0,1:T(8,128)} %get-tuple-element.304, f32[]{:T(128)} %get-tuple-element.306, f32[]{:T(128)} %get-tuple-element.303), kind=kOutput, calls=%fused_computation.4.clone.1 | convolution fusion | flops 1813118976 | bytes 5505032 | tf_op jit(solution)/shard_map/while/body/eval_jaxpr/while/body/dot_general | solution.py:18
  160.2 3.7 %fusion.38 = f32[768,256]{0,1:T(8,128)S(1)} fusion(f32[768,256]{0,1:T(8,128)S(1)} %copy.48, f32[768,256]{0,1:T(8,128)} %get-tuple-element.307, f32[768,768]{1,0:T(8,128)S(1)} %get-tuple-element.305, f32[768,256]{0,1:T(8,128)} %get-tuple-element.304, f32[]{:T(128)} %get-tuple-element.306, f32[]{:T(128)} %get-tuple-element.303), kind=kOutput, calls=%fused_computation.4.clone.1 | convolution fusion | flops 1813118976 | bytes 5505032 | tf_op jit(solution)/shard_map/while/body/eval_jaxpr/while/body/dot_general | solution.py:18
  164.6 3.7 %fusion.38 = f32[768,256]{0,1:T(8,128)S(1)} fusion(f32[768,256]{0,1:T(8,128)S(1)} %copy.48, f32[768,256]{0,1:T(8,128)} %get-tuple-element.307, f32[768,768]{1,0:T(8,128)S(1)} %get-tuple-element.305, f32[768,256]{0,1:T(8,128)} %get-tuple-element.304, f32[]{:T(128)} %get-tuple-element.306, f32[]{:T(128)} %get-tuple-element.303), kind=kOutput, calls=%fused_computation.4.clone.1 | convolution fusion | flops 1813118976 | bytes 5505032 | tf_op jit(solution)/shard_map/while/body/eval_jaxpr/while/body/dot_general | solution.py:18
  168.9 2.9 fusion.34
  173.8 2.1 constant_dynamic-update-slice_fusion.2
  178.8 2.2 fusion.35
  182.8 2.1 constant_dynamic-slice_fusion.5
  184.8 1.4 copy.22
  189.3 13.8 %while.26 = (s32[]{:T(128)}, f32[768,256]{0,1:T(8,128)S(1)}, s32[]{:T(128)}, f32[]{:T(128)}, f32[768,256]{0,1:T(8,128)}, /*index=5*/f32[768,768]{1,0:T(8,128)S(1)}, f32[]{:T(128)}, f32[768,256]{0,1:T(8,128)}, s32[]{:T(128)}) while((s32[]{:T(128)}, f32[768,256]{0,1:T(8,128)S(1)}, s32[]{:T(128)}, f32[]{:T(128)}, f32[768,256]{0,1:T(8,128)}, ...), condition=%wide.region_3.3_spmd, body=%wide.region_2.2_spmd.sunk | while | flops 1813118976 | bytes 7077989 | solution.py:23
  190.0 3.7 %fusion.38 = f32[768,256]{0,1:T(8,128)S(1)} fusion(f32[768,256]{0,1:T(8,128)S(1)} %copy.48, f32[768,256]{0,1:T(8,128)} %get-tuple-element.307, f32[768,768]{1,0:T(8,128)S(1)} %get-tuple-element.305, f32[768,256]{0,1:T(8,128)} %get-tuple-element.304, f32[]{:T(128)} %get-tuple-element.306, f32[]{:T(128)} %get-tuple-element.303), kind=kOutput, calls=%fused_computation.4.clone.1 | convolution fusion | flops 1813118976 | bytes 5505032 | tf_op jit(solution)/shard_map/while/body/eval_jaxpr/while/body/dot_general | solution.py:18
  194.4 3.7 %fusion.38 = f32[768,256]{0,1:T(8,128)S(1)} fusion(f32[768,256]{0,1:T(8,128)S(1)} %copy.48, f32[768,256]{0,1:T(8,128)} %get-tuple-element.307, f32[768,768]{1,0:T(8,128)S(1)} %get-tuple-element.305, f32[768,256]{0,1:T(8,128)} %get-tuple-element.304, f32[]{:T(128)} %get-tuple-element.306, f32[]{:T(128)} %get-tuple-element.303), kind=kOutput, calls=%fused_computation.4.clone.1 | convolution fusion | flops 1813118976 | bytes 5505032 | tf_op jit(solution)/shard_map/while/body/eval_jaxpr/while/body/dot_general | solution.py:18
  198.8 3.7 %fusion.38 = f32[768,256]{0,1:T(8,128)S(1)} fusion(f32[768,256]{0,1:T(8,128)S(1)} %copy.48, f32[768,256]{0,1:T(8,128)} %get-tuple-element.307, f32[768,768]{1,0:T(8,128)S(1)} %get-tuple-element.305, f32[768,256]{0,1:T(8,128)} %get-tuple-element.304, f32[]{:T(128)} %get-tuple-element.306, f32[]{:T(128)} %get-tuple-element.303), kind=kOutput, calls=%fused_computation.4.clone.1 | convolution fusion | flops 1813118976 | bytes 5505032 | tf_op jit(solution)/shard_map/while/body/eval_jaxpr/while/body/dot_general | solution.py:18
  203.1 2.9 fusion.34
  207.9 2.1 constant_dynamic-update-slice_fusion.2
  213.0 2.2 fusion.35
  216.9 2.1 constant_dynamic-slice_fusion.5
  219.0 1.4 copy.22
  223.5 13.8 %while.26 = (s32[]{:T(128)}, f32[768,256]{0,1:T(8,128)S(1)}, s32[]{:T(128)}, f32[]{:T(128)}, f32[768,256]{0,1:T(8,128)}, /*index=5*/f32[768,768]{1,0:T(8,128)S(1)}, f32[]{:T(128)}, f32[768,256]{0,1:T(8,128)}, s32[]{:T(128)}) while((s32[]{:T(128)}, f32[768,256]{0,1:T(8,128)S(1)}, s32[]{:T(128)}, f32[]{:T(128)}, f32[768,256]{0,1:T(8,128)}, ...), condition=%wide.region_3.3_spmd, body=%wide.region_2.2_spmd.sunk | while | flops 1813118976 | bytes 7077989 | solution.py:23
  224.2 3.7 %fusion.38 = f32[768,256]{0,1:T(8,128)S(1)} fusion(f32[768,256]{0,1:T(8,128)S(1)} %copy.48, f32[768,256]{0,1:T(8,128)} %get-tuple-element.307, f32[768,768]{1,0:T(8,128)S(1)} %get-tuple-element.305, f32[768,256]{0,1:T(8,128)} %get-tuple-element.304, f32[]{:T(128)} %get-tuple-element.306, f32[]{:T(128)} %get-tuple-element.303), kind=kOutput, calls=%fused_computation.4.clone.1 | convolution fusion | flops 1813118976 | bytes 5505032 | tf_op jit(solution)/shard_map/while/body/eval_jaxpr/while/body/dot_general | solution.py:18
  228.6 3.7 %fusion.38 = f32[768,256]{0,1:T(8,128)S(1)} fusion(f32[768,256]{0,1:T(8,128)S(1)} %copy.48, f32[768,256]{0,1:T(8,128)} %get-tuple-element.307, f32[768,768]{1,0:T(8,128)S(1)} %get-tuple-element.305, f32[768,256]{0,1:T(8,128)} %get-tuple-element.304, f32[]{:T(128)} %get-tuple-element.306, f32[]{:T(128)} %get-tuple-element.303), kind=kOutput, calls=%fused_computation.4.clone.1 | convolution fusion | flops 1813118976 | bytes 5505032 | tf_op jit(solution)/shard_map/while/body/eval_jaxpr/while/body/dot_general | solution.py:18
  233.0 3.7 %fusion.38 = f32[768,256]{0,1:T(8,128)S(1)} fusion(f32[768,256]{0,1:T(8,128)S(1)} %copy.48, f32[768,256]{0,1:T(8,128)} %get-tuple-element.307, f32[768,768]{1,0:T(8,128)S(1)} %get-tuple-element.305, f32[768,256]{0,1:T(8,128)} %get-tuple-element.304, f32[]{:T(128)} %get-tuple-element.306, f32[]{:T(128)} %get-tuple-element.303), kind=kOutput, calls=%fused_computation.4.clone.1 | convolution fusion | flops 1813118976 | bytes 5505032 | tf_op jit(solution)/shard_map/while/body/eval_jaxpr/while/body/dot_general | solution.py:18
  237.3 2.9 fusion.34
  242.1 2.1 constant_dynamic-update-slice_fusion.2
  246.0 11.4 %psum.14 = f32[2]{0:T(128)S(1)} all-reduce(f32[2]{0:T(128)S(1)} %compare_select_fusion), channel_id=1, replica_groups=mesh['expert'=8,'token'=4] {'token'}, use_global_device_ids=true, to_apply=%region_8.9 | all-reduce | flops 2 | bytes 16 | tf_op jit(solution)/shard_map/psum | solution.py:56
  257.4 55.3 %psum.15 = f32[]{:T(128)} all-reduce(f32[]{:T(128)} %reduce_sum.47), channel_id=1, replica_groups=mesh['expert'=8,'token'=4] {'expert','token'}, use_global_device_ids=true, to_apply=%region_10.11 | all-reduce | flops 1 | bytes 8 | tf_op jit(solution)/shard_map/psum | solution.py:57
  (80 shorter events, 40.5 us)
Async XLA Ops:
  7.2 69.2 %all-gather.2.cloned.1.call-start = ((), (), s32[]{:S(2)}) async-start(), calls=%async_computation | async-start | bytes 3932160 | tf_op jit(solution)/shard_map/all_gather | solution.py:40
  10.1 71.0 %copy-start.1 = (s32[4]{0:T(128)S(1)}, s32[4]{0:T(128)}, u32[]{:S(2)}) copy-start(s32[4]{0:T(128)} %param.14) | copy-start | bytes 52
  10.1 71.0 %copy-start.2 = (f32[4]{0:T(128)S(1)}, f32[4]{0:T(128)}, u32[]{:S(2)}) copy-start(f32[4]{0:T(128)} %param.15) | copy-start | bytes 52
  91.6 0.9 copy-start
  138.9 0.9 copy-start
  186.3 0.9 copy-start
  220.4 0.9 copy-start
Sparse Core Ops, SparseCore 0:
  10.2 66.1 all-gather.1
where the time goes:
time: 323 us; the launch traced here: 321 us
  matrix products  90.8 us (28%)
  blocking collectives  66.7 us (21%)
  waiting for transfers between devices  66.3 us (21%)
  local copies, waits for them, and re-layouts  47.1 us (15%)
  other arithmetic  17.6 us (5%)
  loops' own time  16.9 us (5%)
  between operations  15.4 us (5%)
    dot_general x18, matrix products, advance(): jnp.dot(gram_matrix, current - float_weights, precision=lax.Precision.HIG...  66.3 us
    all_gather x1, waiting for transfers between devices, on_device(): lax.all_gather(masked, 'token', axis=1, tiled=True)  66.2 us
    psum x1, blocking collectives, on_device(): layer_energy = lax.psum(jnp.sum(energies), ('expert', 'token'))  55.3 us
    dynamic_slice x24, local copies, waits for them, and re-layouts, on_device(): lax.map(one_task, (weights, kept_mask, step_counts, ridge_scale))  23.4 us
    dynamic_update_slice x16, local copies, waits for them, and re-layouts, on_device(): lax.map(one_task, (weights, kept_mask, step_counts, ridge_scale))  19.2 us
    another operation x4, loops' own time, solve_task(): result = lax.fori_loop(0, task_count, advance, float_mask * float_weights)  14.3 us
    dot_general x4, matrix products, solve_task(): jnp.dot(gram_matrix, change, precision=lax.Precision.HIGHEST)  11.5 us
    psum x1, blocking collectives, on_device(): expert_terms = lax.psum(picker * jnp.sum(numerators), 'token')  11.4 us
  transfers between devices with their start and end apart: 1, of which 1 were waited for; matrix products, arithmetic and copies ran while one was open for 0% of the time, Pallas kernels for 0%

commit v1 on v0

--- a/solution.py
+++ b/solution.py
@@ -5,6 +5,27 @@
 
 D = 2048
 COLS = 256
+
+
+def collect(x, axis, dim):
+    length, mine, rows = (lax.axis_size(axis), lax.axis_index(axis), x.shape[dim])
+    ahead = [(i, (i + 1) % length) for i in range(length)]
+    backward = [(i, (i - 1) % length) for i in range(length)]
+    out = jnp.zeros((*x.shape[:dim], length * rows, *x.shape[dim + 1 :]), x.dtype)
+    out = lax.dynamic_update_slice_in_dim(out, x, mine * rows, axis=dim)
+    from_left = from_right = x
+    half = length // 2
+    for hop in range(1, half + 1):
+        from_left = lax.ppermute(from_left, axis, ahead)
+        out = lax.dynamic_update_slice_in_dim(
+            out, from_left, (mine - hop) % length * rows, axis=dim
+        )
+        if hop < length - half:
+            from_right = lax.ppermute(from_right, axis, backward)
+            out = lax.dynamic_update_slice_in_dim(
+                out, from_right, (mine + hop) % length * rows, axis=dim
+            )
+    return out
 
 
 def solve_task(gram_matrix, frobenius, task_weights, task_mask, task_count, task_ridge):
@@ -36,9 +57,7 @@
     total_rows = row_count * lax.axis_size("token")
     own_slot = lax.axis_index("token") * local_tasks // per_expert
     masked = activations * routed[:, :, None].astype(jnp.bfloat16)
-    own_rows = lax.dynamic_index_in_dim(
-        lax.all_gather(masked, "token", axis=1, tiled=True), own_slot, 0, keepdims=False
-    )
+    own_rows = lax.dynamic_index_in_dim(collect(masked, "token", 1), own_slot, 0, keepdims=False)
     gram_sum = lax.dot_general(
         own_rows, own_rows, (((0,), (0,)), ((), ())), preferred_element_type=jnp.float32
     )

time: 323 us -> 301 us (0.932)
  waiting for transfers between devices: 66.3 us -> 49.3 us
  between operations: 15.4 us -> 1.92 us
  starting transfers between devices: 0.04 us -> 5.15 us
  local copies, waits for them, and re-layouts: 47.1 us -> 51.9 us
    all_gather x1 -> x0, waiting for transfers between devices: 66.2 us -> none  [on_device(): lax.all_gather(masked, 'token', axis=1, tiled=True)]
    ppermute x0 -> x3, waiting for transfers between devices: none -> 49.3 us  [the longest x2 34.8 us: collect(): from_left = lax.ppermute(from_left, axis, ahead)]
    ppermute x0 -> x3, starting transfers between devices: none -> 5.15 us  [the longest x2 3.08 us: collect(): from_left = lax.ppermute(from_left, axis, ahead)]
  transfers between devices with their start and end apart: 1 -> 3, of which waited for: 1 -> 3; matrix products, arithmetic and copies ran while one was open for 0% -> 1% of each run, Pallas kernels for 0% -> 0%
where the time goes in v1:
time: 301 us; the launch traced here: 299 us
  matrix products  90.8 us (30%)
  blocking collectives  66.7 us (22%)
  local copies, waits for them, and re-layouts  51.9 us (17%)
  waiting for transfers between devices  49.3 us (16%)
  loops' own time  16.9 us (6%)
  other arithmetic  16.6 us (6%)
  starting transfers between devices  5.15 us (2%)
    dot_general x18, matrix products, advance(): jnp.dot(gram_matrix, current - float_weights, precision=lax.Precision.HIG...  66.3 us
    psum x1, blocking collectives, on_device(): layer_energy = lax.psum(jnp.sum(energies), ('expert', 'token'))  55.8 us
    ppermute x2, waiting for transfers between devices, collect(): from_left = lax.ppermute(from_left, axis, ahead)  34.8 us
    dynamic_slice x24, local copies, waits for them, and re-layouts, on_device(): lax.map(one_task, (weights, kept_mask, step_counts, ridge_scale))  23.4 us
    dynamic_update_slice x16, local copies, waits for them, and re-layouts, on_device(): lax.map(one_task, (weights, kept_mask, step_counts, ridge_scale))  19.2 us
    ppermute x1, waiting for transfers between devices, collect(): from_right = lax.ppermute(from_right, axis, backward)  14.6 us
    another operation x4, loops' own time, solve_task(): result = lax.fori_loop(0, task_count, advance, float_mask * float_weights)  14.3 us
    dot_general x4, matrix products, solve_task(): jnp.dot(gram_matrix, change, precision=lax.Precision.HIGHEST)  11.5 us
  transfers between devices with their start and end apart: 3, of which 3 were waited for; matrix products, arithmetic and copies ran while one was open for 1% of the time, Pallas kernels for 0%

profile of v1, /device:TPU:0, one launch (start us, length us, event | category | flops | bytes accessed | tf_op | source)
XLA Modules:
  0.0 299.2 jit_solution(4611825249701073098)
XLA Ops:
  1.4 1.9 broadcast_in_dim.19
  4.3 3.1 %collective-permute-start = (bf16[2,256,768]{2,1,0:T(8,128)(2,1)S(1)}, bf16[2,256,768]{2,1,0:T(8,128)(2,1)S(1)}, u32[]{:S(2)}, u32[]{:S(2)}) collective-permute-start(bf16[2,256,768]{2,1,0:T(8,128)(2,1)S(1)} %get-tuple-element.151), channel_id=1, source_target_pairs={{0,1},{1,2},{2,3},{3,0},{4,5},{5,6},{6,7},{7,4},{8,9},{9,10},{10,1... | collective-permute-start | bytes 2359304 | tf_op jit(solution)/shard_map/ppermute | solution.py:19
  7.4 2.1 collective-permute-start.1
  9.5 18.4 %collective-permute-done = bf16[2,256,768]{2,1,0:T(8,128)(2,1)S(1)} collective-permute-done((bf16[2,256,768]{2,1,0:T(8,128)(2,1)S(1)}, bf16[2,256,768]{2,1,0:T(8,128)(2,1)S(1)}, u32[]{:S(2)}, u32[]{:S(2)}) %collective-permute-start) | collective-permute-done | bytes 786464 | tf_op jit(solution)/shard_map/ppermute | solution.py:19
  28.9 14.6 %collective-permute-done.1 = bf16[2,256,768]{2,1,0:T(8,128)(2,1)S(1)} collective-permute-done((bf16[2,256,768]{2,1,0:T(8,128)(2,1)S(1)}, bf16[2,256,768]{2,1,0:T(8,128)(2,1)S(1)}, u32[]{:S(2)}, u32[]{:S(2)}) %collective-permute-start.1) | collective-permute-done | bytes 786464 | tf_op jit(solution)/shard_map/ppermute | solution.py:24
  44.4 16.4 %collective-permute-done.2 = bf16[2,256,768]{2,1,0:T(8,128)(2,1)S(1)} collective-permute-done((bf16[2,256,768]{2,1,0:T(8,128)(2,1)S(1)}, bf16[2,256,768]{2,1,0:T(8,128)(2,1)S(1)}, u32[]{:S(2)}, u32[]{:S(2)}) %collective-permute-start.2) | collective-permute-done | bytes 786464 | tf_op jit(solution)/shard_map/ppermute | solution.py:19
  61.7 4.1 %multiply_reduce_fusion = (f32[]{:T(128)}, f32[768,768]{1,0:T(8,128)S(1)}) fusion(bf16[2,1024,768]{2,1,0:T(8,128)(2,1)} %constant_dynamic-update-slice_fusion.1, s32[]{:T(128)S(6)} %select_n.43), kind=kOutput, calls=%fused_computation.22 | convolution fusion | flops 1209729024 | bytes 3932168 | tf_op jit(solution)/shard_map/dot_general | solution.py:61
  66.4 163.0 %while.25 = (s32[]{:T(128)}, f32[4,768,256]{2,1,0:T(8,128)}, f32[4]{0:T(128)S(1)}, f32[4]{0:T(128)S(1)}, s32[4,768,256]{2,1,0:T(8,128)}, /*index=5*/bf16[4,768,2...) while((s32[]{:T(128)}, f32[4,768,256]{2,1,0:T(8,128)}, ...), condition=%wide.region_6.7_spmd, body=%wide.region_1.6_spmd.sunk | while | flops 5439750144 | bytes 29491652 | solution.py:71
  69.4 2.2 fusion.35
  73.4 2.1 constant_dynamic-slice_fusion.5
  79.9 27.0 %while.26 = (s32[]{:T(128)}, f32[768,256]{0,1:T(8,128)S(1)}, s32[]{:T(128)}, f32[]{:T(128)}, f32[768,256]{0,1:T(8,128)}, /*index=5*/f32[768,768]{1,0:T(8,128)S(1)}, f32[]{:T(128)}, f32[768,256]{0,1:T(8,128)}, s32[]{:T(128)}) while((s32[]{:T(128)}, f32[768,256]{0,1:T(8,128)S(1)}, s32[]{:T(128)}, f32[]{:T(128)}, f32[768,256]{0,1:T(8,128)}, ...), condition=%wide.region_3.3_spmd, body=%wide.region_2.2_spmd.sunk | while | flops 1813118976 | bytes 7077989 | solution.py:44
  80.6 3.7 %fusion.38 = f32[768,256]{0,1:T(8,128)S(1)} fusion(f32[768,256]{0,1:T(8,128)S(1)} %copy.52, f32[768,256]{0,1:T(8,128)} %get-tuple-element.309, f32[768,768]{1,0:T(8,128)S(1)} %get-tuple-element.307, f32[768,256]{0,1:T(8,128)} %get-tuple-element.306, f32[]{:T(128)} %get-tuple-element.308, f32[]{:T(128)} %get-tuple-element.305), kind=kOutput, calls=%fused_computation.4.clone.1 | convolution fusion | flops 1813118976 | bytes 5505032 | tf_op jit(solution)/shard_map/while/body/eval_jaxpr/while/body/dot_general | solution.py:39
  85.0 3.7 %fusion.38 = f32[768,256]{0,1:T(8,128)S(1)} fusion(f32[768,256]{0,1:T(8,128)S(1)} %copy.52, f32[768,256]{0,1:T(8,128)} %get-tuple-element.309, f32[768,768]{1,0:T(8,128)S(1)} %get-tuple-element.307, f32[768,256]{0,1:T(8,128)} %get-tuple-element.306, f32[]{:T(128)} %get-tuple-element.308, f32[]{:T(128)} %get-tuple-element.305), kind=kOutput, calls=%fused_computation.4.clone.1 | convolution fusion | flops 1813118976 | bytes 5505032 | tf_op jit(solution)/shard_map/while/body/eval_jaxpr/while/body/dot_general | solution.py:39
  89.4 3.7 %fusion.38 = f32[768,256]{0,1:T(8,128)S(1)} fusion(f32[768,256]{0,1:T(8,128)S(1)} %copy.52, f32[768,256]{0,1:T(8,128)} %get-tuple-element.309, f32[768,768]{1,0:T(8,128)S(1)} %get-tuple-element.307, f32[768,256]{0,1:T(8,128)} %get-tuple-element.306, f32[]{:T(128)} %get-tuple-element.308, f32[]{:T(128)} %get-tuple-element.305), kind=kOutput, calls=%fused_computation.4.clone.1 | convolution fusion | flops 1813118976 | bytes 5505032 | tf_op jit(solution)/shard_map/while/body/eval_jaxpr/while/body/dot_general | solution.py:39
  93.8 3.7 %fusion.38 = f32[768,256]{0,1:T(8,128)S(1)} fusion(f32[768,256]{0,1:T(8,128)S(1)} %copy.52, f32[768,256]{0,1:T(8,128)} %get-tuple-element.309, f32[768,768]{1,0:T(8,128)S(1)} %get-tuple-element.307, f32[768,256]{0,1:T(8,128)} %get-tuple-element.306, f32[]{:T(128)} %get-tuple-element.308, f32[]{:T(128)} %get-tuple-element.305), kind=kOutput, calls=%fused_computation.4.clone.1 | convolution fusion | flops 1813118976 | bytes 5505032 | tf_op jit(solution)/shard_map/while/body/eval_jaxpr/while/body/dot_general | solution.py:39
  98.2 3.7 %fusion.38 = f32[768,256]{0,1:T(8,128)S(1)} fusion(f32[768,256]{0,1:T(8,128)S(1)} %copy.52, f32[768,256]{0,1:T(8,128)} %get-tuple-element.309, f32[768,768]{1,0:T(8,128)S(1)} %get-tuple-element.307, f32[768,256]{0,1:T(8,128)} %get-tuple-element.306, f32[]{:T(128)} %get-tuple-element.308, f32[]{:T(128)} %get-tuple-element.305), kind=kOutput, calls=%fused_computation.4.clone.1 | convolution fusion | flops 1813118976 | bytes 5505032 | tf_op jit(solution)/shard_map/while/body/eval_jaxpr/while/body/dot_general | solution.py:39
  102.6 3.7 %fusion.38 = f32[768,256]{0,1:T(8,128)S(1)} fusion(f32[768,256]{0,1:T(8,128)S(1)} %copy.52, f32[768,256]{0,1:T(8,128)} %get-tuple-element.309, f32[768,768]{1,0:T(8,128)S(1)} %get-tuple-element.307, f32[768,256]{0,1:T(8,128)} %get-tuple-element.306, f32[]{:T(128)} %get-tuple-element.308, f32[]{:T(128)} %get-tuple-element.305), kind=kOutput, calls=%fused_computation.4.clone.1 | convolution fusion | flops 1813118976 | bytes 5505032 | tf_op jit(solution)/shard_map/while/body/eval_jaxpr/while/body/dot_general | solution.py:39
  106.9 2.9 fusion.34
  111.7 2.1 constant_dynamic-update-slice_fusion.6
  116.8 2.2 fusion.35
  120.7 2.1 constant_dynamic-slice_fusion.5
  127.3 27.0 %while.26 = (s32[]{:T(128)}, f32[768,256]{0,1:T(8,128)S(1)}, s32[]{:T(128)}, f32[]{:T(128)}, f32[768,256]{0,1:T(8,128)}, /*index=5*/f32[768,768]{1,0:T(8,128)S(1)}, f32[]{:T(128)}, f32[768,256]{0,1:T(8,128)}, s32[]{:T(128)}) while((s32[]{:T(128)}, f32[768,256]{0,1:T(8,128)S(1)}, s32[]{:T(128)}, f32[]{:T(128)}, f32[768,256]{0,1:T(8,128)}, ...), condition=%wide.region_3.3_spmd, body=%wide.region_2.2_spmd.sunk | while | flops 1813118976 | bytes 7077989 | solution.py:44
  128.0 3.7 %fusion.38 = f32[768,256]{0,1:T(8,128)S(1)} fusion(f32[768,256]{0,1:T(8,128)S(1)} %copy.52, f32[768,256]{0,1:T(8,128)} %get-tuple-element.309, f32[768,768]{1,0:T(8,128)S(1)} %get-tuple-element.307, f32[768,256]{0,1:T(8,128)} %get-tuple-element.306, f32[]{:T(128)} %get-tuple-element.308, f32[]{:T(128)} %get-tuple-element.305), kind=kOutput, calls=%fused_computation.4.clone.1 | convolution fusion | flops 1813118976 | bytes 5505032 | tf_op jit(solution)/shard_map/while/body/eval_jaxpr/while/body/dot_general | solution.py:39
  132.4 3.7 %fusion.38 = f32[768,256]{0,1:T(8,128)S(1)} fusion(f32[768,256]{0,1:T(8,128)S(1)} %copy.52, f32[768,256]{0,1:T(8,128)} %get-tuple-element.309, f32[768,768]{1,0:T(8,128)S(1)} %get-tuple-element.307, f32[768,256]{0,1:T(8,128)} %get-tuple-element.306, f32[]{:T(128)} %get-tuple-element.308, f32[]{:T(128)} %get-tuple-element.305), kind=kOutput, calls=%fused_computation.4.clone.1 | convolution fusion | flops 1813118976 | bytes 5505032 | tf_op jit(solution)/shard_map/while/body/eval_jaxpr/while/body/dot_general | solution.py:39
  136.8 3.7 %fusion.38 = f32[768,256]{0,1:T(8,128)S(1)} fusion(f32[768,256]{0,1:T(8,128)S(1)} %copy.52, f32[768,256]{0,1:T(8,128)} %get-tuple-element.309, f32[768,768]{1,0:T(8,128)S(1)} %get-tuple-element.307, f32[768,256]{0,1:T(8,128)} %get-tuple-element.306, f32[]{:T(128)} %get-tuple-element.308, f32[]{:T(128)} %get-tuple-element.305), kind=kOutput, calls=%fused_computation.4.clone.1 | convolution fusion | flops 1813118976 | bytes 5505032 | tf_op jit(solution)/shard_map/while/body/eval_jaxpr/while/body/dot_general | solution.py:39
  141.2 3.7 %fusion.38 = f32[768,256]{0,1:T(8,128)S(1)} fusion(f32[768,256]{0,1:T(8,128)S(1)} %copy.52, f32[768,256]{0,1:T(8,128)} %get-tuple-element.309, f32[768,768]{1,0:T(8,128)S(1)} %get-tuple-element.307, f32[768,256]{0,1:T(8,128)} %get-tuple-element.306, f32[]{:T(128)} %get-tuple-element.308, f32[]{:T(128)} %get-tuple-element.305), kind=kOutput, calls=%fused_computation.4.clone.1 | convolution fusion | flops 1813118976 | bytes 5505032 | tf_op jit(solution)/shard_map/while/body/eval_jaxpr/while/body/dot_general | solution.py:39
  145.5 3.7 %fusion.38 = f32[768,256]{0,1:T(8,128)S(1)} fusion(f32[768,256]{0,1:T(8,128)S(1)} %copy.52, f32[768,256]{0,1:T(8,128)} %get-tuple-element.309, f32[768,768]{1,0:T(8,128)S(1)} %get-tuple-element.307, f32[768,256]{0,1:T(8,128)} %get-tuple-element.306, f32[]{:T(128)} %get-tuple-element.308, f32[]{:T(128)} %get-tuple-element.305), kind=kOutput, calls=%fused_computation.4.clone.1 | convolution fusion | flops 1813118976 | bytes 5505032 | tf_op jit(solution)/shard_map/while/body/eval_jaxpr/while/body/dot_general | solution.py:39
  149.9 3.7 %fusion.38 = f32[768,256]{0,1:T(8,128)S(1)} fusion(f32[768,256]{0,1:T(8,128)S(1)} %copy.52, f32[768,256]{0,1:T(8,128)} %get-tuple-element.309, f32[768,768]{1,0:T(8,128)S(1)} %get-tuple-element.307, f32[768,256]{0,1:T(8,128)} %get-tuple-element.306, f32[]{:T(128)} %get-tuple-element.308, f32[]{:T(128)} %get-tuple-element.305), kind=kOutput, calls=%fused_computation.4.clone.1 | convolution fusion | flops 1813118976 | bytes 5505032 | tf_op jit(solution)/shard_map/while/body/eval_jaxpr/while/body/dot_general | solution.py:39
  154.3 2.9 fusion.34
  159.1 2.1 constant_dynamic-update-slice_fusion.6
  164.1 2.2 fusion.35
  168.1 2.1 constant_dynamic-slice_fusion.5
  174.6 13.8 %while.26 = (s32[]{:T(128)}, f32[768,256]{0,1:T(8,128)S(1)}, s32[]{:T(128)}, f32[]{:T(128)}, f32[768,256]{0,1:T(8,128)}, /*index=5*/f32[768,768]{1,0:T(8,128)S(1)}, f32[]{:T(128)}, f32[768,256]{0,1:T(8,128)}, s32[]{:T(128)}) while((s32[]{:T(128)}, f32[768,256]{0,1:T(8,128)S(1)}, s32[]{:T(128)}, f32[]{:T(128)}, f32[768,256]{0,1:T(8,128)}, ...), condition=%wide.region_3.3_spmd, body=%wide.region_2.2_spmd.sunk | while | flops 1813118976 | bytes 7077989 | solution.py:44
  175.3 3.7 %fusion.38 = f32[768,256]{0,1:T(8,128)S(1)} fusion(f32[768,256]{0,1:T(8,128)S(1)} %copy.52, f32[768,256]{0,1:T(8,128)} %get-tuple-element.309, f32[768,768]{1,0:T(8,128)S(1)} %get-tuple-element.307, f32[768,256]{0,1:T(8,128)} %get-tuple-element.306, f32[]{:T(128)} %get-tuple-element.308, f32[]{:T(128)} %get-tuple-element.305), kind=kOutput, calls=%fused_computation.4.clone.1 | convolution fusion | flops 1813118976 | bytes 5505032 | tf_op jit(solution)/shard_map/while/body/eval_jaxpr/while/body/dot_general | solution.py:39
  179.7 3.7 %fusion.38 = f32[768,256]{0,1:T(8,128)S(1)} fusion(f32[768,256]{0,1:T(8,128)S(1)} %copy.52, f32[768,256]{0,1:T(8,128)} %get-tuple-element.309, f32[768,768]{1,0:T(8,128)S(1)} %get-tuple-element.307, f32[768,256]{0,1:T(8,128)} %get-tuple-element.306, f32[]{:T(128)} %get-tuple-element.308, f32[]{:T(128)} %get-tuple-element.305), kind=kOutput, calls=%fused_computation.4.clone.1 | convolution fusion | flops 1813118976 | bytes 5505032 | tf_op jit(solution)/shard_map/while/body/eval_jaxpr/while/body/dot_general | solution.py:39
  184.1 3.7 %fusion.38 = f32[768,256]{0,1:T(8,128)S(1)} fusion(f32[768,256]{0,1:T(8,128)S(1)} %copy.52, f32[768,256]{0,1:T(8,128)} %get-tuple-element.309, f32[768,768]{1,0:T(8,128)S(1)} %get-tuple-element.307, f32[768,256]{0,1:T(8,128)} %get-tuple-element.306, f32[]{:T(128)} %get-tuple-element.308, f32[]{:T(128)} %get-tuple-element.305), kind=kOutput, calls=%fused_computation.4.clone.1 | convolution fusion | flops 1813118976 | bytes 5505032 | tf_op jit(solution)/shard_map/while/body/eval_jaxpr/while/body/dot_general | solution.py:39
  188.4 2.9 fusion.34
  193.2 2.1 constant_dynamic-update-slice_fusion.6
  198.3 2.2 fusion.35
  202.2 2.1 constant_dynamic-slice_fusion.5
  208.8 13.8 %while.26 = (s32[]{:T(128)}, f32[768,256]{0,1:T(8,128)S(1)}, s32[]{:T(128)}, f32[]{:T(128)}, f32[768,256]{0,1:T(8,128)}, /*index=5*/f32[768,768]{1,0:T(8,128)S(1)}, f32[]{:T(128)}, f32[768,256]{0,1:T(8,128)}, s32[]{:T(128)}) while((s32[]{:T(128)}, f32[768,256]{0,1:T(8,128)S(1)}, s32[]{:T(128)}, f32[]{:T(128)}, f32[768,256]{0,1:T(8,128)}, ...), condition=%wide.region_3.3_spmd, body=%wide.region_2.2_spmd.sunk | while | flops 1813118976 | bytes 7077989 | solution.py:44
  209.5 3.7 %fusion.38 = f32[768,256]{0,1:T(8,128)S(1)} fusion(f32[768,256]{0,1:T(8,128)S(1)} %copy.52, f32[768,256]{0,1:T(8,128)} %get-tuple-element.309, f32[768,768]{1,0:T(8,128)S(1)} %get-tuple-element.307, f32[768,256]{0,1:T(8,128)} %get-tuple-element.306, f32[]{:T(128)} %get-tuple-element.308, f32[]{:T(128)} %get-tuple-element.305), kind=kOutput, calls=%fused_computation.4.clone.1 | convolution fusion | flops 1813118976 | bytes 5505032 | tf_op jit(solution)/shard_map/while/body/eval_jaxpr/while/body/dot_general | solution.py:39
  213.9 3.7 %fusion.38 = f32[768,256]{0,1:T(8,128)S(1)} fusion(f32[768,256]{0,1:T(8,128)S(1)} %copy.52, f32[768,256]{0,1:T(8,128)} %get-tuple-element.309, f32[768,768]{1,0:T(8,128)S(1)} %get-tuple-element.307, f32[768,256]{0,1:T(8,128)} %get-tuple-element.306, f32[]{:T(128)} %get-tuple-element.308, f32[]{:T(128)} %get-tuple-element.305), kind=kOutput, calls=%fused_computation.4.clone.1 | convolution fusion | flops 1813118976 | bytes 5505032 | tf_op jit(solution)/shard_map/while/body/eval_jaxpr/while/body/dot_general | solution.py:39
  218.3 3.7 %fusion.38 = f32[768,256]{0,1:T(8,128)S(1)} fusion(f32[768,256]{0,1:T(8,128)S(1)} %copy.52, f32[768,256]{0,1:T(8,128)} %get-tuple-element.309, f32[768,768]{1,0:T(8,128)S(1)} %get-tuple-element.307, f32[768,256]{0,1:T(8,128)} %get-tuple-element.306, f32[]{:T(128)} %get-tuple-element.308, f32[]{:T(128)} %get-tuple-element.305), kind=kOutput, calls=%fused_computation.4.clone.1 | convolution fusion | flops 1813118976 | bytes 5505032 | tf_op jit(solution)/shard_map/while/body/eval_jaxpr/while/body/dot_general | solution.py:39
  222.6 2.9 fusion.34
  227.4 2.1 constant_dynamic-update-slice_fusion.6
  231.3 11.0 %psum.14 = f32[2]{0:T(128)S(1)} all-reduce(f32[2]{0:T(128)S(1)} %compare_select_fusion), channel_id=1, replica_groups=mesh['expert'=8,'token'=4] {'token'}, use_global_device_ids=true, to_apply=%region_8.9 | all-reduce | flops 2 | bytes 16 | tf_op jit(solution)/shard_map/psum | solution.py:75
  242.3 55.8 %psum.15 = f32[]{:T(128)} all-reduce(f32[]{:T(128)} %reduce_sum.47), channel_id=1, replica_groups=mesh['expert'=8,'token'=4] {'expert','token'}, use_global_device_ids=true, to_apply=%region_10.11 | all-reduce | flops 1 | bytes 8 | tf_op jit(solution)/shard_map/psum | solution.py:76
  (89 shorter events, 50.0 us)
Async XLA Ops:
  0.6 2.6 copy-start.1
  4.3 23.6 %collective-permute-start = (bf16[2,256,768]{2,1,0:T(8,128)(2,1)S(1)}, bf16[2,256,768]{2,1,0:T(8,128)(2,1)S(1)}, u32[]{:S(2)}, u32[]{:S(2)}) collective-permute-start(bf16[2,256,768]{2,1,0:T(8,128)(2,1)S(1)} %get-tuple-element.151), channel_id=1, source_target_pairs={{0,1},{1,2},{2,3},{3,0},{4,5},{5,6},{6,7},{7,4},{8,9},{9,10},{10,1... | collective-permute-start | bytes 2359304 | tf_op jit(solution)/shard_map/ppermute | solution.py:19
  7.4 36.1 %collective-permute-start.1 = (bf16[2,256,768]{2,1,0:T(8,128)(2,1)S(1)}, bf16[2,256,768]{2,1,0:T(8,128)(2,1)S(1)}, u32[]{:S(2)}, u32[]{:S(2)}) collective-permute-start(bf16[2,256,768]{2,1,0:T(8,128)(2,1)S(1)} %get-tuple-element.151), channel_id=1, source_target_pairs={{0,3},{1,0},{2,1},{3,2},{4,7},{5,4},{6,5},{7,6},{8,11},{9,8},{10,9... | collective-permute-start | bytes 2359304 | tf_op jit(solution)/shard_map/ppermute | solution.py:24
  27.9 32.8 %collective-permute-start.2 = (bf16[2,256,768]{2,1,0:T(8,128)(2,1)S(1)}, bf16[2,256,768]{2,1,0:T(8,128)(2,1)S(1)}, u32[]{:S(2)}, u32[]{:S(2)}) collective-permute-start(bf16[2,256,768]{2,1,0:T(8,128)(2,1)S(1)} %collective-permute-done), channel_id=1, source_target_pairs={{0,1},{1,2},{2,3},{3,0},{4,5},{5,6},{6,7},{7,4},{8,9},{9,10},{10,1... | collective-permute-start | bytes 2359304 | tf_op jit(solution)/shard_map/ppermute | solution.py:19
  44.4 22.0 %copy-start.2 = (s32[4]{0:T(128)S(1)}, s32[4]{0:T(128)}, u32[]{:S(2)}) copy-start(s32[4]{0:T(128)} %param.14) | copy-start | bytes 52
  44.4 22.0 %copy-start.3 = (f32[4]{0:T(128)S(1)}, f32[4]{0:T(128)}, u32[]{:S(2)}) copy-start(f32[4]{0:T(128)} %param.15) | copy-start | bytes 52
  76.9 0.9 copy-start
  124.2 0.9 copy-start
  171.6 0.9 copy-start
  205.7 0.9 copy-start
